TPU v7x, 256 devices: a whole 4x4x8 slice. The times are simulated.
256 devices in a mesh: inner: 16 (over x, y), outer: 16 (over z, core).
Axes of the slice: x: 4, y: 4, z: 8, core: 2. Of those that a mesh axis runs over, the one named last changes fastest.
Arguments:
- jac: float32 [4096, 256, 256], P(('outer', 'inner')), may hold values from -0.5 to 1
- obs: float32 [4096, 256], P(('outer', 'inner')), may hold values from -6 to 6
- gain_filter: float32 [256], replicated, may hold values from 0 to 0.1
- gain_smooth: float32 [256, 256], replicated, may hold values from -0.5 to 1
- init_mean: float32 [256], replicated, may hold values from -6 to 6
Outputs:
- filtered: float32 [4096, 256], P(('outer', 'inner'))
- smoothed: float32 [4096, 256], P(('outer', 'inner'))
All inputs are finite; a program needn't handle non-finite values.
Results may differ from a plain program's by a relative error of at most 0.0003.
Values sent between devices are 32-bit elements; how exact they have to be, the bound alone decides.
No kernel may reach another device: no remote copies, remote signals or barrier semaphores. Data moves between devices by JAX's collectives and lax.ppermute only.
A program may use at most 64 MiB of HBM per device.

v0:
```python
import jax
import jax.numpy as jnp
from jax import lax
from jax.sharding import PartitionSpec as P

HIGHEST = lax.Precision.HIGHEST


def entering(part, axis, combine, identity, reverse):
    count = lax.axis_size(axis)
    place = lax.axis_index(axis)
    ahead = count - 1 - place if reverse else place
    gathered = lax.all_gather(part, axis)
    state = jnp.zeros_like(part) + jnp.asarray(identity, part.dtype)

    def one(turn, state):
        source = count - 1 - turn if reverse else turn
        return combine(state, lax.dynamic_index_in_dim(gathered, source, 0, False))

    return lax.fori_loop(0, ahead, one, state)


def last_row(state_width):
    return (jnp.arange(state_width + 1) == state_width).astype(jnp.float32)[:, None]


def identity_map(state_width):
    return jnp.concatenate(
        [jnp.eye(state_width, dtype=jnp.float32), jnp.zeros((1, state_width), jnp.float32)], 0
    )


def compose(earlier, later):
    state_width = later.shape[1]
    product = jnp.dot(earlier, later[:state_width], precision=HIGHEST)
    return product + last_row(state_width) * later[state_width][None, :]


def advance(packed, state):
    state_width = packed.shape[1]
    return jnp.dot(state, packed[:state_width], precision=HIGHEST) + packed[state_width]


def raise_power(factor, count):
    result = jnp.eye(factor.shape[0], dtype=jnp.float32)
    square = factor
    while count > 0:
        if count % 2 == 1:
            result = jnp.dot(result, square, precision=HIGHEST)
        count = count // 2
        if count > 0:
            square = jnp.dot(square, square, precision=HIGHEST)
    return result


def incoming_state(own_map, boundary, reverse):
    state_width = own_map.shape[1]
    identity = identity_map(state_width)
    inner_count = lax.axis_size("inner")
    inner_here = lax.axis_index("inner")
    gathered = lax.all_gather(own_map[None], "inner", axis=0, tiled=True)

    def absorb(running, inputs):
        before, group_total = running
        segment, position = inputs
        group_total = compose(group_total, segment)
        if reverse:
            taken = position > inner_here
        else:
            taken = position < inner_here
        before = jnp.where(taken, group_total, before)
        return ((before, group_total), None)

    (seg_before, group_total), _ = lax.scan(
        absorb,
        (identity, identity),
        (gathered, jnp.arange(inner_count, dtype=jnp.int32)),
        reverse=reverse,
    )
    group_before = entering(group_total, "outer", compose, identity, reverse)
    group_state = advance(group_before, boundary)
    return advance(seg_before, group_state)


def shards(jac, obs, gain_filter, gain_smooth, init_mean):
    state_width = jac.shape[1]
    step_count = jac.shape[0]
    retain = 1.0 - gain_filter
    bottom = last_row(state_width)

    def compose_forward(packed, inputs):
        step_matrix, measured = inputs
        moved = (
            lax.dot_general(packed, step_matrix, (((1,), (1,)), ((), ())), precision=HIGHEST)
            * retain[None, :]
        )
        return (moved + bottom * (gain_filter * measured)[None, :], None)

    forward_map, _ = lax.scan(compose_forward, identity_map(state_width), (jac, obs))
    start_state = incoming_state(forward_map, init_mean, False)

    def forward(state, inputs):
        step_matrix, measured = inputs
        predicted = jnp.dot(step_matrix, state, precision=HIGHEST)
        updated = predicted + gain_filter * (measured - predicted)
        return (updated, (predicted, updated))

    _, (predicted_all, filtered_all) = lax.scan(forward, start_state, (jac, obs))
    correction = filtered_all - predicted_all

    def backward(state, term):
        renewed = jnp.dot(gain_smooth, state, precision=HIGHEST) + term
        return (renewed, renewed)

    zero_state = jnp.zeros((state_width,), jnp.float32)
    offset_sum, _ = lax.scan(backward, zero_state, correction, reverse=True)
    step_power = raise_power(gain_smooth.T, step_count)
    backward_map = jnp.concatenate([step_power, offset_sum[None]], 0)
    after_state = incoming_state(backward_map, zero_state, True)
    _, back_states = lax.scan(backward, after_state, correction, reverse=True)
    return (filtered_all, predicted_all + back_states)


def solution(mesh):
    return jax.shard_map(
        shards,
        mesh=mesh,
        in_specs=(P(("outer", "inner"), None, None), P(("outer", "inner"), None), P(), P(), P()),
        out_specs=(P(("outer", "inner"), None), P(("outer", "inner"), None)),
        check_vma=False,
    )
```

profile of v0, /device:TPU:2, one launch (start us, length us, event | category | flops | bytes accessed | tf_op | source)
XLA Modules:
  0.0 473.1 jit_solution(15027441515699616519)
XLA Ops:
  8.0 34.7 %while.112 = (s32[]{:T(128)}, f32[257,256]{1,0:T(8,128)S(1)}, f32[16,256,256]{2,1,0:T(8,128)}, f32[256]{0:T(256)S(1)}, f32[256]{0:T(256)}, /*index=5*/f32[16,256]{1,0:T(8,128)}, s32[]{:T(128)}) while((s32[]{:T(128)}, f32[257,256]{1,0:T(8,128)S(1)}, f32[16,256,256]{2,1,0:T(8,128)}, f32[256]{0:T(256)S(1)}, f32[256]{0:T(256)}, ...), condition=%wide.region_1.2_spmd.clone, body=%wide.region_0.1_spmd.clone.sunk | while | flops 202311168 | bytes 1322585 | solution.py:99
  13.1 1.4 fusion.105
  19.6 1.4 fusion.105
  26.1 1.4 fusion.105
  32.6 1.4 fusion.105
  39.1 1.4 fusion.105
  43.5 60.2 %all-gather.13.cloned.1.call-done = f32[16,257,256]{2,1,0:T(8,128)} async-done(((f32[1,257,256]{2,1,0:T(8,128)}), f32[16,257,256]{2,1,0:T(8,128)}) %all-gather.13.cloned.1.call-update) | async-done | bytes 4210704 | tf_op jit(solution)/shard_map/all_gather | solution.py:61
  103.8 55.9 %while.106 = (s32[]{:T(128)}, f32[257,256]{1,0:T(8,128)S(1)}, f32[257,256]{1,0:T(8,128)S(1)}, s32[16]{0:T(128)S(1)}, s32[]{:T(128)}, /*index=5*/f32[16,257,256]{2,1,0:T(8,128)}, s32[]{:T(128)}, s32[]{:T(128)}, s32[]{}) while((s32[]{:T(128)}, f32[257,256]{1,0:T(8,128)S(1)}, f32[257,256]{1,0:T(8,128)S(1)}, s32[16]{0:T(128)S(1)}, s32[]{:T(128)}, ...), condition=%wide.region_3.4_spmd, body=%wide.region_2.3_spmd.sunk | while | flops 202310912 | bytes 1846927 | solution.py:74
  105.8 1.5 broadcast_select_fusion.6
  109.3 1.5 broadcast_select_fusion.6
  112.8 1.5 broadcast_select_fusion.6
  116.2 1.5 broadcast_select_fusion.6
  119.7 1.5 broadcast_select_fusion.6
  123.2 1.5 broadcast_select_fusion.6
  126.7 1.5 broadcast_select_fusion.6
  130.2 1.5 broadcast_select_fusion.6
  133.7 1.5 broadcast_select_fusion.6
  137.2 1.5 broadcast_select_fusion.6
  140.7 1.5 broadcast_select_fusion.6
  144.2 1.5 broadcast_select_fusion.6
  147.7 1.5 broadcast_select_fusion.6
  151.2 1.5 broadcast_select_fusion.6
  154.7 1.5 broadcast_select_fusion.6
  158.2 1.5 broadcast_select_fusion.6
  162.6 40.0 %all-gather.15.cloned.1.call-done = f32[16,257,256]{2,1,0:T(8,128)} async-done(((f32[1,257,256]{2,1,0:T(8,128)}), f32[16,257,256]{2,1,0:T(8,128)}) %all-gather.15.cloned.1.call-update) | async-done | bytes 4210704 | tf_op jit(solution)/shard_map/all_gather | solution.py:13
  203.1 33.3 %while.108 = (s32[]{:T(128)}, f32[256]{0:T(256)S(1)}, f32[16,256]{1,0:T(8,128)S(1)}, f32[16,256]{1,0:T(8,128)S(1)}, f32[16,256,256]{2,1,0:T(8,128)}, /*index=5*/...) while((s32[]{:T(128)}, f32[256]{0:T(256)S(1)}, f32[16,256]{1,0:T(8,128)S(1)}, ...), condition=%wide.region_7.8_spmd, body=%wide.region_6.7_spmd.sunk | while | flops 787202 | bytes 275049 | solution.py:108
  236.4 6.1 %while.113 = (s32[]{:T(128)}, f32[256]{0:T(256)S(1)}, f32[256,256]{1,0:T(8,128)S(1)}, f32[16,256]{1,0:T(8,128)S(1)}, s32[]{:T(128)}, /*index=5*/s32[]{:T(128)}, s32[]{:T(128)}) while((s32[]{:T(128)}, f32[256]{0:T(256)S(1)}, f32[256,256]{1,0:T(8,128)S(1)}, f32[16,256]{1,0:T(8,128)S(1)}, s32[]{:T(128)}, /*index=5*/s32[]{:T(128)}, ...), condition=%wide.region_9.10_spmd.clone, body=%wide.region_8.9_spmd.clone.sunk | while | flops 786948 | bytes 271463 | solution.py:116
  243.4 86.6 %all-gather.17.cloned.1.call-done = f32[16,257,256]{2,1,0:T(8,128)} async-done(((f32[1,257,256]{2,1,0:T(8,128)}), f32[16,257,256]{2,1,0:T(8,128)}) %all-gather.17.cloned.1.call-update) | async-done | bytes 4210704 | tf_op jit(solution)/shard_map/all_gather | solution.py:61
  330.0 54.4 %while.109 = (s32[]{:T(128)}, f32[257,256]{1,0:T(8,128)S(1)}, f32[257,256]{1,0:T(8,128)S(1)}, s32[16]{0:T(128)S(1)}, s32[]{:T(128)}, /*index=5*/f32[16,257,256]{2,1,0:T(8,128)}, s32[]{:T(128)}, s32[]{:T(128)}, s32[]{:T(128)}, s32[]{}) while((s32[]{:T(128)}, f32[257,256]{1,0:T(8,128)S(1)}, f32[257,256]{1,0:T(8,128)S(1)}, s32[16]{0:T(128)S(1)}, ...), condition=%wide.region_11.12_spmd, body=%wide.region_10.11_spmd.sunk | while | flops 202310912 | bytes 1846439 | solution.py:74
  331.8 1.5 broadcast_select_fusion.7
  335.2 1.5 broadcast_select_fusion.7
  338.6 1.5 broadcast_select_fusion.7
  342.0 1.5 broadcast_select_fusion.7
  345.5 1.5 broadcast_select_fusion.7
  348.9 1.5 broadcast_select_fusion.7
  352.3 1.5 broadcast_select_fusion.7
  355.7 1.5 broadcast_select_fusion.7
  359.1 1.5 broadcast_select_fusion.7
  362.5 1.5 broadcast_select_fusion.7
  365.9 1.5 broadcast_select_fusion.7
  369.3 1.5 broadcast_select_fusion.7
  372.7 1.5 broadcast_select_fusion.7
  376.1 1.5 broadcast_select_fusion.7
  379.5 1.5 broadcast_select_fusion.7
  382.9 1.5 broadcast_select_fusion.7
  385.1 42.2 %all-gather.19.cloned.1.call-done = f32[16,257,256]{2,1,0:T(8,128)} async-done(((f32[1,257,256]{2,1,0:T(8,128)}), f32[16,257,256]{2,1,0:T(8,128)}) %all-gather.19.cloned.1.call-update) | async-done | bytes 4210704 | tf_op jit(solution)/shard_map/all_gather | solution.py:13
  427.3 31.8 %while.110 = (s32[]{:T(128)}, f32[257,256]{1,0:T(8,128)S(1)}, s32[]{:T(128)}, f32[16,257,256]{2,1,0:T(8,128)}, s32[]{:T(128)}, /*index=5*/s32[]{:T(128)}, s32[]{:T(128)}, s32[]{:T(128)}, s32[]{}) while((s32[]{:T(128)}, f32[257,256]{1,0:T(8,128)S(1)}, s32[]{:T(128)}, f32[16,257,256]{2,1,0:T(8,128)}, s32[]{:T(128)}, /*index=5*/s32[]{:T(128)}, ...), condition=%wide.region_13.14_spmd, body=%wide.region_12.13_spmd.sunk | while | flops 202245120 | bytes 1320107 | solution.py:20
  459.6 6.3 %while.111 = (s32[]{:T(128)}, f32[256]{0:T(256)S(1)}, f32[16,256]{1,0:T(8,128)S(1)}, f32[256,256]{1,0:T(8,128)S(1)}, f32[16,256]{1,0:T(8,128)S(1)}, /*index=5*/s32[]{:T(128)}, s32[]{:T(128)}, s32[]{:T(128)}) while((s32[]{:T(128)}, f32[256]{0:T(256)S(1)}, f32[16,256]{1,0:T(8,128)S(1)}, f32[256,256]{1,0:T(8,128)S(1)}, ...), condition=%wide.region_15.16_spmd, body=%wide.region_14.15_spmd.sunk | while | flops 786691 | bytes 271465 | solution.py:120
  (513 shorter events, 152.2 us)
Async XLA Ops:
  7.2 195.4 %copy-start = (f32[256]{0:T(256)S(1)}, f32[256]{0:T(256)}, u32[]{:S(2)}) copy-start(f32[256]{0:T(256)} %param.25) | copy-start | bytes 3076
  7.2 96.6 %all-gather.13.cloned.1.call-start = ((), (), s32[]{:S(2)}) async-start(), calls=%async_computation | async-start | bytes 4595712 | tf_op jit(solution)/shard_map/all_gather | solution.py:61
  42.7 0.7 copy-start.4
  43.4 159.2 %all-gather.15.cloned.1.call-start = ((), (), s32[]{:S(2)}) async-start(), calls=%async_computation.1 | async-start | bytes 4595712 | tf_op jit(solution)/shard_map/all_gather | solution.py:13
  103.8 56.7 %copy-start.1 = (f32[256,256]{1,0:T(8,128)S(1)}, f32[256,256]{1,0:T(8,128)}, u32[]{:S(2)}) copy-start(f32[256,256]{1,0:T(8,128)} %param.24) | copy-start | bytes 786436
  159.7 0.7 copy-start.2
  160.4 169.6 %all-gather.17.cloned.1.call-start = ((), (), s32[]{:S(2)}) async-start(), calls=%async_computation.2 | async-start | bytes 4595712 | tf_op jit(solution)/shard_map/all_gather | solution.py:61
  161.9 41.2 %copy-start.5 = (f32[256]{0:T(256)S(1)}, f32[256]{0:T(256)}, u32[]{:S(2)}) copy-start(f32[256]{0:T(256)} %get-tuple-element.1116) | copy-start | bytes 3076
  236.4 93.5 %copy-start.6 = (f32[16,256]{1,0:T(8,128)}, f32[16,256]{1,0:T(8,128)S(1)}, u32[]{:S(2)}) copy-start(f32[16,256]{1,0:T(8,128)S(1)} %get-tuple-element.497) | copy-start | bytes 49156
  243.3 184.0 %all-gather.19.cloned.1.call-start = ((), (), s32[]{:S(2)}) async-start(), calls=%async_computation.3 | async-start | bytes 4595712 | tf_op jit(solution)/shard_map/all_gather | solution.py:13
  384.4 0.7 copy-start.3
Sparse Core Ops, SparseCore 0:
  43.5 60.1 all-gather.12
  160.5 42.0 all-gather.14
  243.4 86.5 all-gather.16
  385.3 42.0 all-gather.18
where the time goes:
time: 479 us; the launch traced here: 473 us
  waiting for transfers between devices  229 us (48%)
  matrix products  121 us (25%)
  local copies, waits for them, and re-layouts  70.9 us (15%)
  loops' own time  23.3 us (5%)
  other arithmetic  14.7 us (3%)
  between operations  14.1 us (3%)
    all_gather x2, waiting for transfers between devices, incoming_state(): gathered = lax.all_gather(own_map[None], 'inner', axis=0, tiled=True)  147 us
    all_gather x2, waiting for transfers between devices, entering(): gathered = lax.all_gather(part, axis)  82.2 us
    dot_general x47, matrix products, compose(): product = jnp.dot(earlier, later[:state_width], precision=HIGHEST)  68 us
    slice x47, local copies, waits for them, and re-layouts, compose(): return product + last_row(state_width) * later[state_width][None, :]  33.1 us
    dot_general x16, matrix products, compose_forward(): lax.dot_general(packed, step_matrix, (((1,), (1,)), ((), ())), precision=...  21.9 us
    another operation x2, loops' own time, incoming_state(): lax.scan(absorb, (identity, identity), (gathered, jnp.arange(inner_count,...  20.8 us
    dot_general x16, matrix products, forward(): predicted = jnp.dot(step_matrix, state, precision=HIGHEST)  19.6 us
    dynamic_slice x32, local copies, waits for them, and re-layouts, incoming_state(): lax.scan(absorb, (identity, identity), (gathered, jnp.arange(inner_count,...  18.6 us
  transfers between devices with their start and end apart: 4, of which 4 were waited for; matrix products, arithmetic and copies ran while one was open for 0% of the time, Pallas kernels for 0%

commit v1 on v0

--- a/solution.py
+++ b/solution.py
@@ -58,7 +58,9 @@
     identity = identity_map(state_width)
     inner_count = lax.axis_size("inner")
     inner_here = lax.axis_index("inner")
-    gathered = lax.all_gather(own_map[None], "inner", axis=0, tiled=True)
+    gathered = jnp.concatenate(
+        lax.all_to_all(jnp.stack([own_map[None]] * lax.axis_size("inner")), "inner", 0, 0), axis=0
+    )
 
     def absorb(running, inputs):
         before, group_total = running

time: 479 us -> 527 us (1.10)
  local copies, waits for them, and re-layouts: 70.9 us -> 87.8 us
  waiting for transfers between devices: 229 us -> 245 us
  starting transfers between devices: 0.16 us -> 14.8 us
    all_gather x2 -> x0, waiting for transfers between devices: 147 us -> none  [incoming_state(): gathered = lax.all_gather(own_map[None], 'inner', axis=0, tiled=True)]
    all_to_all x0 -> x2, waiting for transfers between devices: none -> 109 us  [incoming_state(): lax.all_to_all(jnp.stack([own_map[None]] * lax.axis_size('inner')), 'inne...]
    all_gather x2, waiting for transfers between devices: 82.2 us -> 136 us  [entering(): gathered = lax.all_gather(part, axis)]
    all_to_all x0 -> x2, starting transfers between devices: none -> 14.8 us  [incoming_state(): lax.all_to_all(jnp.stack([own_map[None]] * lax.axis_size('inner')), 'inne...]
    reshape x0 -> x2, local copies, waits for them, and re-layouts: none -> 9.29 us  [incoming_state(): jnp.concatenate(lax.all_to_all(jnp.stack([own_map[None]] * lax.axis_size(...]
    another operation x3 -> x5, local copies, waits for them, and re-layouts: 0.06 us -> 8.3 us  [the longest x2 8.24 us: incoming_state(): jnp.stack([own_map[None]] * lax.axis_size('inner'))]
where the time goes in v1:
time: 527 us; the launch traced here: 520 us
  waiting for transfers between devices  245 us (46%)
  matrix products  121 us (23%)
  local copies, waits for them, and re-layouts  87.8 us (17%)
  loops' own time  23.3 us (4%)
  starting transfers between devices  14.8 us (3%)
  between operations  14.4 us (3%)
  other arithmetic  14.1 us (3%)
    all_gather x2, waiting for transfers between devices, entering(): gathered = lax.all_gather(part, axis)  136 us
    all_to_all x2, waiting for transfers between devices, incoming_state(): lax.all_to_all(jnp.stack([own_map[None]] * lax.axis_size('inner')), 'inne...  109 us
    dot_general x47, matrix products, compose(): product = jnp.dot(earlier, later[:state_width], precision=HIGHEST)  68.2 us
    slice x47, local copies, waits for them, and re-layouts, compose(): return product + last_row(state_width) * later[state_width][None, :]  33.2 us
    dot_general x16, matrix products, compose_forward(): lax.dot_general(packed, step_matrix, (((1,), (1,)), ((), ())), precision=...  21.9 us
    another operation x2, loops' own time, incoming_state(): lax.scan(absorb, (identity, identity), (gathered, jnp.arange(inner_count,...  20.8 us
    dot_general x16, matrix products, forward(): predicted = jnp.dot(step_matrix, state, precision=HIGHEST)  19.6 us
    dynamic_slice x32, local copies, waits for them, and re-layouts, incoming_state(): lax.scan(absorb, (identity, identity), (gathered, jnp.arange(inner_count,...  18.6 us
  transfers between devices with their start and end apart: 4, of which 4 were waited for; matrix products, arithmetic and copies ran while one was open for 0% of the time, Pallas kernels for 0%

profile of v1, /device:TPU:2, one launch (start us, length us, event | category | flops | bytes accessed | tf_op | source)
XLA Modules:
  0.0 520.3 jit_solution(11222014332758654666)
XLA Ops:
  8.0 34.6 %while.112 = (s32[]{:T(128)}, f32[257,256]{1,0:T(8,128)S(1)}, f32[16,256,256]{2,1,0:T(8,128)}, f32[256]{0:T(256)S(1)}, f32[256]{0:T(256)}, /*index=5*/f32[16,256]{1,0:T(8,128)}, s32[]{:T(128)}) while((s32[]{:T(128)}, f32[257,256]{1,0:T(8,128)S(1)}, f32[16,256,256]{2,1,0:T(8,128)}, f32[256]{0:T(256)S(1)}, f32[256]{0:T(256)}, ...), condition=%wide.region_1.2_spmd.clone, body=%wide.region_0.1_spmd.clone.sunk | while | flops 202311168 | bytes 1322585 | solution.py:101
  42.6 4.1 stack.6
  46.8 7.5 %all-to-all-start = ((f32[16,1,257,256]{3,1,2,0:T(1,128)}), f32[16,1,257,256]{3,1,2,0:T(1,128)}, u32[]{:S(2)}, u32[]{:S(2)}) async-start(f32[16,1,257,256]{3,1,2,0:T(1,128)} %stack.6), calls=%async_computation | async-start | bytes 8421376 | tf_op jit(solution)/shard_map/all_to_all | solution.py:62
  54.4 54.3 %all-to-all-done = f32[16,1,257,256]{3,1,2,0:T(1,128)} async-done(((f32[16,1,257,256]{3,1,2,0:T(1,128)}), f32[16,1,257,256]{3,1,2,0:T(1,128)}, u32[]{:S(2)}, u32[]{:S(2)}) %all-to-all-start) | async-done | bytes 4210720 | tf_op jit(solution)/shard_map/all_to_all | solution.py:62
  108.7 4.6 copy.16
  113.3 56.0 %while.106 = (s32[]{:T(128)}, f32[257,256]{1,0:T(8,128)S(1)}, f32[257,256]{1,0:T(8,128)S(1)}, s32[16]{0:T(128)S(1)}, s32[]{:T(128)}, /*index=5*/f32[16,257,256]{2,1,0:T(8,128)}, s32[]{:T(128)}, s32[]{:T(128)}, s32[]{}) while((s32[]{:T(128)}, f32[257,256]{1,0:T(8,128)S(1)}, f32[257,256]{1,0:T(8,128)S(1)}, s32[16]{0:T(128)S(1)}, s32[]{:T(128)}, ...), condition=%wide.region_3.4_spmd, body=%wide.region_2.3_spmd.sunk | while | flops 202310912 | bytes 1846927 | solution.py:76
  115.4 1.5 broadcast_select_fusion.6
  118.9 1.5 broadcast_select_fusion.6
  122.4 1.5 broadcast_select_fusion.6
  125.9 1.5 broadcast_select_fusion.6
  129.4 1.5 broadcast_select_fusion.6
  132.8 1.5 broadcast_select_fusion.6
  136.3 1.5 broadcast_select_fusion.6
  139.8 1.5 broadcast_select_fusion.6
  143.3 1.5 broadcast_select_fusion.6
  146.8 1.5 broadcast_select_fusion.6
  153.8 1.5 broadcast_select_fusion.6
  157.3 1.5 broadcast_select_fusion.6
  160.8 1.5 broadcast_select_fusion.6
  164.3 1.5 broadcast_select_fusion.6
  167.8 1.5 broadcast_select_fusion.6
  172.2 54.8 %all-gather.7.cloned.1.call-done = f32[16,257,256]{2,1,0:T(8,128)} async-done(((f32[1,257,256]{2,1,0:T(8,128)}), f32[16,257,256]{2,1,0:T(8,128)}) %all-gather.7.cloned.1.call-update) | async-done | bytes 4210704 | tf_op jit(solution)/shard_map/all_gather | solution.py:13
  227.5 33.3 %while.108 = (s32[]{:T(128)}, f32[256]{0:T(256)S(1)}, f32[16,256]{1,0:T(8,128)S(1)}, f32[16,256]{1,0:T(8,128)S(1)}, f32[16,256,256]{2,1,0:T(8,128)}, /*index=5*/...) while((s32[]{:T(128)}, f32[256]{0:T(256)S(1)}, f32[16,256]{1,0:T(8,128)S(1)}, ...), condition=%wide.region_7.8_spmd, body=%wide.region_6.7_spmd.sunk | while | flops 787202 | bytes 275049 | solution.py:110
  260.9 6.1 %while.113 = (s32[]{:T(128)}, f32[256]{0:T(256)S(1)}, f32[256,256]{1,0:T(8,128)S(1)}, f32[16,256]{1,0:T(8,128)S(1)}, s32[]{:T(128)}, /*index=5*/s32[]{:T(128)}, s32[]{:T(128)}) while((s32[]{:T(128)}, f32[256]{0:T(256)S(1)}, f32[256,256]{1,0:T(8,128)S(1)}, f32[16,256]{1,0:T(8,128)S(1)}, s32[]{:T(128)}, /*index=5*/s32[]{:T(128)}, ...), condition=%wide.region_9.10_spmd.clone, body=%wide.region_8.9_spmd.clone.sunk | while | flops 786948 | bytes 271463 | solution.py:118
  267.0 4.1 stack.7
  271.1 7.3 %all-to-all-start.1 = ((f32[16,1,257,256]{3,1,2,0:T(1,128)}), f32[16,1,257,256]{3,1,2,0:T(1,128)}, u32[]{:S(2)}, u32[]{:S(2)}) async-start(f32[16,1,257,256]{3,1,2,0:T(1,128)} %stack.7), calls=%async_computation.1 | async-start | bytes 8421376 | tf_op jit(solution)/shard_map/all_to_all | solution.py:62
  278.5 54.2 %all-to-all-done.1 = f32[16,1,257,256]{3,1,2,0:T(1,128)} async-done(((f32[16,1,257,256]{3,1,2,0:T(1,128)}), f32[16,1,257,256]{3,1,2,0:T(1,128)}, u32[]{:S(2)}, u32[]{:S(2)}) %all-to-all-start.1) | async-done | bytes 4210720 | tf_op jit(solution)/shard_map/all_to_all | solution.py:62
  332.7 4.6 copy.15
  337.4 54.6 %while.109 = (s32[]{:T(128)}, f32[257,256]{1,0:T(8,128)S(1)}, f32[257,256]{1,0:T(8,128)S(1)}, s32[16]{0:T(128)S(1)}, s32[]{:T(128)}, /*index=5*/f32[16,257,256]{2,1,0:T(8,128)}, s32[]{:T(128)}, s32[]{:T(128)}, s32[]{:T(128)}, s32[]{}) while((s32[]{:T(128)}, f32[257,256]{1,0:T(8,128)S(1)}, f32[257,256]{1,0:T(8,128)S(1)}, s32[16]{0:T(128)S(1)}, ...), condition=%wide.region_11.12_spmd, body=%wide.region_10.11_spmd.sunk | while | flops 202310912 | bytes 1846439 | solution.py:76
  339.3 1.5 broadcast_select_fusion.7
  342.7 1.5 broadcast_select_fusion.7
  346.1 1.5 broadcast_select_fusion.7
  349.5 1.5 broadcast_select_fusion.7
  352.9 1.5 broadcast_select_fusion.7
  356.4 1.5 broadcast_select_fusion.7
  359.8 1.5 broadcast_select_fusion.7
  363.2 1.5 broadcast_select_fusion.7
  366.6 1.5 broadcast_select_fusion.7
  370.0 1.5 broadcast_select_fusion.7
  373.4 1.5 broadcast_select_fusion.7
  376.8 1.5 broadcast_select_fusion.7
  380.2 1.5 broadcast_select_fusion.7
  383.7 1.5 broadcast_select_fusion.7
  387.1 1.5 broadcast_select_fusion.7
  390.5 1.5 broadcast_select_fusion.7
  392.7 81.5 %all-gather.9.cloned.1.call-done = f32[16,257,256]{2,1,0:T(8,128)} async-done(((f32[1,257,256]{2,1,0:T(8,128)}), f32[16,257,256]{2,1,0:T(8,128)}) %all-gather.9.cloned.1.call-update) | async-done | bytes 4210704 | tf_op jit(solution)/shard_map/all_gather | solution.py:13
  474.2 31.8 %while.110 = (s32[]{:T(128)}, f32[257,256]{1,0:T(8,128)S(1)}, s32[]{:T(128)}, f32[16,257,256]{2,1,0:T(8,128)}, s32[]{:T(128)}, /*index=5*/s32[]{:T(128)}, s32[]{:T(128)}, s32[]{:T(128)}, s32[]{}) while((s32[]{:T(128)}, f32[257,256]{1,0:T(8,128)S(1)}, s32[]{:T(128)}, f32[16,257,256]{2,1,0:T(8,128)}, s32[]{:T(128)}, /*index=5*/s32[]{:T(128)}, ...), condition=%wide.region_13.14_spmd, body=%wide.region_12.13_spmd.sunk | while | flops 202245120 | bytes 1320107 | solution.py:20
  506.5 6.4 %while.111 = (s32[]{:T(128)}, f32[256]{0:T(256)S(1)}, f32[16,256]{1,0:T(8,128)S(1)}, f32[256,256]{1,0:T(8,128)S(1)}, f32[16,256]{1,0:T(8,128)S(1)}, /*index=5*/s32[]{:T(128)}, s32[]{:T(128)}, s32[]{:T(128)}) while((s32[]{:T(128)}, f32[256]{0:T(256)S(1)}, f32[16,256]{1,0:T(8,128)S(1)}, f32[256,256]{1,0:T(8,128)S(1)}, ...), condition=%wide.region_15.16_spmd, body=%wide.region_14.15_spmd.sunk | while | flops 786691 | bytes 271465 | solution.py:122
  (518 shorter events, 159.1 us)
Async XLA Ops:
  7.2 219.8 %copy-start = (f32[256]{0:T(256)S(1)}, f32[256]{0:T(256)}, u32[]{:S(2)}) copy-start(f32[256]{0:T(256)} %param.25) | copy-start | bytes 3076
  7.2 271.2 %copy-start.1 = (f32[257,256]{1,0:T(8,128)}, f32[257,256]{1,0:T(8,128)S(1)}, u32[]{:S(2)}) copy-start(f32[257,256]{1,0:T(8,128)S(1)} %pad_convert_fusion) | copy-start | bytes 789508
  46.8 61.9 %all-to-all-start = ((f32[16,1,257,256]{3,1,2,0:T(1,128)}), f32[16,1,257,256]{3,1,2,0:T(1,128)}, u32[]{:S(2)}, u32[]{:S(2)}) async-start(f32[16,1,257,256]{3,1,2,0:T(1,128)} %stack.6), calls=%async_computation | async-start | bytes 8421376 | tf_op jit(solution)/shard_map/all_to_all | solution.py:62
  54.2 172.8 %all-gather.7.cloned.1.call-start = ((), (), s32[]{:S(2)}) async-start(), calls=%async_computation.2 | async-start | bytes 4595712 | tf_op jit(solution)/shard_map/all_gather | solution.py:13
  113.3 56.8 %copy-start.5 = (f32[256,256]{1,0:T(8,128)S(1)}, f32[256,256]{1,0:T(8,128)}, u32[]{:S(2)}) copy-start(f32[256,256]{1,0:T(8,128)} %param.24) | copy-start | bytes 786436
  169.3 0.7 copy-start.6
  171.5 56.0 %copy-start.7 = (f32[256]{0:T(256)S(1)}, f32[256]{0:T(256)}, u32[]{:S(2)}) copy-start(f32[256]{0:T(256)} %get-tuple-element.1124) | copy-start | bytes 3076
  260.8 10.2 %copy-start.8 = (f32[16,256]{1,0:T(8,128)}, f32[16,256]{1,0:T(8,128)S(1)}, u32[]{:S(2)}) copy-start(f32[16,256]{1,0:T(8,128)S(1)} %get-tuple-element.497) | copy-start | bytes 49156
  271.1 61.6 %all-to-all-start.1 = ((f32[16,1,257,256]{3,1,2,0:T(1,128)}), f32[16,1,257,256]{3,1,2,0:T(1,128)}, u32[]{:S(2)}, u32[]{:S(2)}) async-start(f32[16,1,257,256]{3,1,2,0:T(1,128)} %stack.7), calls=%async_computation.1 | async-start | bytes 8421376 | tf_op jit(solution)/shard_map/all_to_all | solution.py:62
  278.4 195.9 %all-gather.9.cloned.1.call-start = ((), (), s32[]{:S(2)}) async-start(), calls=%async_computation.3 | async-start | bytes 4595712 | tf_op jit(solution)/shard_map/all_gather | solution.py:13
  278.4 58.9 %copy-start.4 = (f32[257,256]{1,0:T(8,128)S(1)}, f32[257,256]{1,0:T(8,128)}, u32[]{:S(2)}) copy-start(f32[257,256]{1,0:T(8,128)} %copy-done.1) | copy-start | bytes 789508
  337.3 136.9 %copy-start.2 = (f32[257,256]{1,0:T(8,128)S(1)}, f32[257,256]{1,0:T(8,128)}, u32[]{:S(2)}) copy-start(f32[257,256]{1,0:T(8,128)} %copy-done.1) | copy-start | bytes 789508
  392.0 0.7 copy-start.3
Sparse Core Ops, SparseCore 0:
  170.2 56.7 all-gather.6
  392.8 81.3 all-gather.8
